TPU v7x, 256 devices: a whole 4x4x8 slice. The times are simulated.
256 devices in a mesh: rep: 16 (over z, core), rows: 16 (over y, x).
Axes of the slice: x: 4, y: 4, z: 8, core: 2. Of those that a mesh axis runs over, the one named last changes fastest.
Arguments:
- weights: bfloat16 [7168, 2048], P('rows'), may hold values from -6 to 6
- momentum: float32 [16, 7168, 2048], P('rep', 'rows'), may hold values from -8 to 8
- gradient: bfloat16 [16, 7168, 2048], P('rep', 'rows'), may hold values from -8 to 8
- right_factor: float32 [2048, 512], P('rows'), may hold values from -6 to 6
Outputs:
- new_weights: bfloat16 [7168, 2048], P('rows')
- new_momentum: float32 [16, 7168, 2048], P('rep', 'rows')
- new_right: float32 [2048, 512], P('rows')
All inputs are finite; a program needn't handle non-finite values.
Results may differ from a plain program's by a relative error of at most 0.019.
Values may be sent and summed in bfloat16 or wider, within the bound.
No kernel may reach another device: no remote copies, remote signals or barrier semaphores. Data moves between devices by JAX's collectives and lax.ppermute only.
A program may use at most 64 MiB of HBM per device.

v0:
```python
import jax
import jax.numpy as jnp
from jax import lax
from jax.sharding import Mesh
from jax.sharding import PartitionSpec as P

M = 7168
N = 2048
ROWS = ("rows_0", "rows_1")
momentum_keep = 0.05
learn_rate = 0.5
tiny = 1e-06


def from_everyone(value, axis):
    size = lax.axis_size(axis)
    return lax.all_to_all(
        jnp.broadcast_to(value[None], (size, *value.shape)), axis, 0, 0, tiled=True
    )


def laid_out(blocks, dim):
    dims = list(blocks.shape[1:])
    dims[dim] *= blocks.shape[0]
    return jnp.moveaxis(blocks, 0, dim).reshape(dims)


def gather_directly(value, axis, dim):
    blocks = from_everyone(value, axis)
    return laid_out(blocks, dim)


def gathered_total(value, axis):
    return lax.all_gather(value, axis).astype(jnp.float32).sum(0)


def sum_by_axis(terms, axes):
    running = terms.astype(jnp.bfloat16)
    for axis in axes:
        running = lax.psum_scatter(running, axis, scatter_dimension=0, tiled=True)
    return running.astype(jnp.float32)


def over_axes(value, axes):
    for axis in axes:
        value = lax.psum(value, axis)
    return value


def per_device(weights, momentum, gradient, right_factor):
    groups = lax.axis_size("rep")
    combined = momentum[0] + gradient[0].astype(jnp.float32)
    combined_half = combined.astype(jnp.bfloat16)
    columns = combined.shape[1]
    block = combined_half
    left_local = jnp.dot(
        block,
        gather_directly(right_factor.astype(jnp.bfloat16), ROWS, 0),
        preferred_element_type=jnp.float32,
    )
    left_local = lax.optimization_barrier(left_local.astype(jnp.bfloat16)).astype(jnp.float32)
    left_mean = gathered_total(left_local.astype(jnp.bfloat16), "rep").astype(jnp.float32) / groups
    gram = lax.psum(jnp.dot(left_mean.T, left_mean, precision=lax.Precision.HIGHEST), ROWS)
    chol = jnp.linalg.cholesky(gram)
    left_orth = jax.scipy.linalg.solve_triangular(chol, left_mean.T, lower=True).T
    left_half = left_orth.astype(jnp.bfloat16)
    block = combined_half
    right_part = sum_by_axis(
        jnp.einsum("ij,ik->jk", block, left_half, preferred_element_type=jnp.float32), ROWS
    )
    right_mean = gathered_total(right_part.astype(jnp.bfloat16), "rep").astype(jnp.float32) / groups
    squares = over_axes(jnp.sum(right_mean * right_mean, axis=0), ROWS)
    new_right = right_mean / jnp.sqrt(squares / columns + tiny)
    stacked = jnp.stack([right_mean.astype(jnp.bfloat16), new_right.astype(jnp.bfloat16)], 0)
    both = jnp.einsum(
        "ir,skr->sik",
        left_half,
        lax.all_gather(stacked, ROWS, axis=1, tiled=True),
        preferred_element_type=jnp.float32,
    )
    feedback = both[0]
    update = both[1]
    new_momentum = combined - momentum_keep * feedback
    new_weights = (weights.astype(jnp.float32) - learn_rate * jnp.sqrt(M / N) * update).astype(
        jnp.bfloat16
    )
    return (new_weights, new_momentum[None], new_right)


def solution(mesh):
    split = Mesh(mesh.devices.reshape(mesh.shape["rep"], 4, 4), ("rep", "rows_0", "rows_1"))
    in_specs = (P(ROWS, None), P("rep", ROWS, None), P("rep", ROWS, None), P(ROWS, None))
    out_specs = (P(ROWS, None), P("rep", ROWS, None), P(ROWS, None))
    return jax.shard_map(
        per_device, mesh=split, in_specs=in_specs, out_specs=out_specs, check_vma=False
    )
```

profile of v0, /device:TPU:1, one launch (start us, length us, event | category | flops | bytes accessed | tf_op | source)
XLA Modules:
  0.0 543.4 jit_solution(8520991013041620438)
XLA Ops:
  7.2 1.1 convert_element_type.64
  8.4 0.2 broadcast_in_dim.3
  8.6 34.8 %all_to_all.5 = bf16[16,128,512]{2,1,0:T(8,128)(2,1)S(1)} all-to-all(bf16[16,128,512]{2,1,0:T(8,128)(2,1)S(1)} %broadcast_in_dim.3), channel_id=1, replica_groups=mesh['rep'=16,'rows_0'=4,'rows_1'=4] {'rows_0','rows_1'}, dimensions={0} | all-to-all | bytes 4194304 | tf_op jit(solution)/shard_map/all_to_all | solution.py:17
  43.3 1.9 convolution_convert_fusion.1
  45.4 51.9 %all-gather.8.cloned.1.call-done = bf16[7168,512]{1,0:T(8,128)(2,1)} async-done(((bf16[448,512]{1,0:T(8,128)(2,1)}), bf16[7168,512]{1,0:T(8,128)(2,1)}) %all-gather.8.cloned.1.call-update) | async-done | bytes 7340048 | tf_op jit(solution)/shard_map/all_gather | solution.py:34
  97.2 4.2 convert_reduce_fusion
  101.4 2.9 fusion.7
  104.4 0.5 reduce-scatter.3.cloned.1.call-start
  104.9 1.0 multiply_bitcast_fusion
  105.9 92.8 %all-reduce.3.cloned.1.call-done = f32[512,512]{0,1:T(8,128)} async-done(((f32[512,512]{0,1:T(8,128)}), f32[512,512]{0,1:T(8,128)}) %all-reduce.3.cloned.1.call-update) | async-done | bytes 1048592 | tf_op jit(solution)/shard_map/psum | solution.py:63
  198.7 1.6 copy.8
  200.3 1.4 fusion.6
  201.8 1.0 copy-done.4
  202.7 11.7 %cholesky.104 = f32[128,128]{1,0:T(8,128)S(1)} custom-call(f32[128,128]{1,0:T(8,128)S(1)} %cholesky.266), custom_call_target="Cholesky" | custom-call | tf_op jit(solution)/shard_map/jit(cholesky)/cholesky | solution.py:64
  214.5 9.8 %custom-call.31 = f32[1,128,128]{1,2,0:T(8,128)S(1)} custom-call(f32[1,128,128]{2,1,0:T(8,128)S(1)} %get-tuple-element.32), custom_call_target="InvertDiagBlocksLowerTriangular" | custom-call | tf_op jit(solution)/shard_map/jit(cholesky)/cholesky | solution.py:64
  224.3 0.1 cholesky.224
  224.4 1.2 constant_dynamic-update-slice_fusion.3
  225.7 1.3 convolution_subtract_fusion.3
  227.0 11.7 %cholesky.217 = f32[128,128]{1,0:T(8,128)S(1)} custom-call(f32[128,128]{1,0:T(8,128)S(1)} %cholesky.270), custom_call_target="Cholesky" | custom-call | tf_op jit(solution)/shard_map/jit(cholesky)/cholesky | solution.py:64
  238.7 10.0 %custom-call.32 = f32[1,128,128]{1,2,0:T(8,128)S(1)} custom-call(f32[1,128,128]{2,1,0:T(8,128)S(1)} %get-tuple-element.29), custom_call_target="InvertDiagBlocksLowerTriangular" | custom-call | tf_op jit(solution)/shard_map/jit(cholesky)/cholesky | solution.py:64
  248.7 0.3 convolution_dynamic-update-slice_fusion
  248.9 1.3 convolution_subtract_fusion.4
  250.2 11.7 %cholesky.238 = f32[128,128]{1,0:T(8,128)S(1)} custom-call(f32[128,128]{1,0:T(8,128)S(1)} %cholesky.275), custom_call_target="Cholesky" | custom-call | tf_op jit(solution)/shard_map/jit(cholesky)/cholesky | solution.py:64
  262.0 0.7 compare_reduce_fusion.1
  262.7 9.8 %custom-call.33 = f32[1,128,128]{1,2,0:T(8,128)S(1)} custom-call(f32[1,128,128]{2,1,0:T(8,128)S(1)} %get-tuple-element.26), custom_call_target="InvertDiagBlocksLowerTriangular" | custom-call | tf_op jit(solution)/shard_map/jit(cholesky)/cholesky | solution.py:64
  272.5 0.2 convolution_dynamic-update-slice_fusion.1
  272.7 1.2 convolution_subtract_fusion.5
  273.9 11.7 %cholesky.255 = f32[128,128]{1,0:T(8,128)S(1)} custom-call(f32[128,128]{1,0:T(8,128)S(1)} %convolution_subtract_fusion.5), custom_call_target="Cholesky" | custom-call | tf_op jit(solution)/shard_map/jit(cholesky)/cholesky | solution.py:64
  285.7 0.6 compare_reduce_fusion
  286.3 0.9 compare_reduce_fusion.2
  289.7 1.1 select_select_fusion
  290.8 11.7 %while.1 = (s32[]{:T(128)}, f32[512,512]{1,0:T(8,128)}, s32[4,2]{0,1:T(2,128)S(1)}, f32[4,128,128]{2,1,0:T(8,128)S(1)}, s32[]{:T(128)}) while((s32[]{:T(128)}, f32[512,512]{1,0:T(8,128)}, s32[4,2]{0,1:T(2,128)S(1)}, f32[4,128,128]{2,1,0:T(8,128)S(1)}, s32[]{:T(128)}) %tuple.35), condition=%wide.while_cond, body=%wide.while_body.sunk | while | flops 2 | bytes 131189 | solution.py:65
  290.8 0.1 constant_dynamic-slice_fusion.2
  290.9 0.6 fusion.57
  291.5 2.2 bitcast_dynamic-update-slice_fusion.2
  293.8 0.1 constant_dynamic-slice_fusion.2
  293.9 0.6 fusion.57
  294.5 2.2 bitcast_dynamic-update-slice_fusion.2
  296.8 0.6 fusion.57
  297.4 2.2 bitcast_dynamic-update-slice_fusion.2
  299.7 0.1 constant_dynamic-slice_fusion.2
  299.7 0.6 fusion.57
  300.3 2.2 bitcast_dynamic-update-slice_fusion.2
  302.5 39.3 %custom-call.34 = f32[4,128,128]{1,2,0:T(8,128)S(1)} custom-call(f32[4,128,128]{2,1,0:T(8,128)S(1)} %get-tuple-element.10), custom_call_target="InvertDiagBlocksLowerTriangular" | custom-call | tf_op jit(solution)/shard_map/jit(_solve_triangular)/triangular_solve | solution.py:65
  341.9 1.4 fusion.48
  343.3 1.3 convolution_subtract_fusion.2
  344.6 0.3 fusion.47
  345.0 1.5 convolution_subtract_fusion.1
  346.5 0.3 fusion.46
  346.9 1.8 convolution_subtract_fusion
  348.7 0.3 convolution_convert_fusion.2
  349.0 2.7 convolution_convert_fusion
  351.8 33.1 %reduce-scatter.3.cloned.1.call-done = bf16[512,512]{1,0:T(8,128)(2,1)} async-done(((bf16[2048,512]{1,0:T(8,128)(2,1)}), bf16[512,512]{1,0:T(8,128)(2,1)}) %reduce-scatter.3.cloned.1.call-update) | async-done | bytes 524304 | tf_op jit(solution)/shard_map/reduce_scatter | solution.py:40
  385.0 23.9 %reduce-scatter.5.cloned.1.call-done = bf16[128,512]{1,0:T(8,128)(2,1)} async-done(((bf16[512,512]{1,0:T(8,128)(2,1)}), bf16[128,512]{1,0:T(8,128)(2,1)}) %reduce-scatter.5.cloned.1.call-update) | async-done | bytes 131088 | tf_op jit(solution)/shard_map/reduce_scatter | solution.py:40
  409.0 43.6 %all-gather.10.cloned.1.call-done = bf16[2048,512]{1,0:T(8,128)(2,1)} async-done(((bf16[128,512]{1,0:T(8,128)(2,1)}), bf16[2048,512]{1,0:T(8,128)(2,1)}) %all-gather.10.cloned.1.call-update) | async-done | bytes 2097168 | tf_op jit(solution)/shard_map/all_gather | solution.py:34
  452.6 1.9 convert_reduce_fusion.1
  454.6 8.5 %psum.22 = f32[512]{0:T(512)S(1)} all-reduce(f32[512]{0:T(512)S(1)} %multiply_reduce_fusion), channel_id=1, replica_groups=mesh['rep'=16,'rows_0'=4,'rows_1'=4] {'rows_0'}, use_global_device_ids=true, to_apply=%region_14.15 | all-reduce | flops 512 | bytes 4096 | tf_op jit(solution)/shard_map/psum | solution.py:46
  463.0 8.4 %psum.23 = f32[512]{0:T(512)S(1)} all-reduce(f32[512]{0:T(512)S(1)} %psum.22), channel_id=1, replica_groups=mesh['rep'=16,'rows_0'=4,'rows_1'=4] {'rows_1'}, use_global_device_ids=true, to_apply=%region_15.16 | all-reduce | flops 512 | bytes 4096 | tf_op jit(solution)/shard_map/psum | solution.py:46
  471.5 0.7 multiply_divide_fusion
  472.2 0.7 pad_maximum_fusion.1
  473.0 54.2 %all-gather.6.cloned.1.call-done = bf16[2,2048,512]{2,1,0:T(8,128)(2,1)} async-done(((bf16[2,128,512]{2,1,0:T(8,128)(2,1)}), bf16[2,2048,512]{2,1,0:T(8,128)(2,1)}) %all-gather.6.cloned.1.call-update) | async-done | bytes 4194320 | tf_op jit(solution)/shard_map/all_gather | solution.py:78
  527.1 4.4 convolution_bitcast_fusion
  531.6 2.8 fusion
  534.5 1.9 fusion.3
  (36 shorter events, 0.7 us)
Async XLA Ops:
  7.2 36.2 %copy-start.3 = (bf16[1,448,2048]{2,1,0:T(8,128)(2,1)S(1)}, bf16[1,448,2048]{2,1,0:T(8,128)(2,1)}, u32[]{:S(2)}) copy-start(bf16[1,448,2048]{2,1,0:T(8,128)(2,1)} %param.6) | copy-start | bytes 5505028
  7.2 90.1 %all-gather.8.cloned.1.call-start = ((), (), s32[]{:S(2)}) async-start(), calls=%async_computation.7 | async-start | bytes 7798784 | tf_op jit(solution)/shard_map/all_gather | solution.py:34
  7.2 36.1 %copy-start = (f32[1,448,2048]{2,1,0:T(8,128)S(1)}, f32[1,448,2048]{2,1,0:T(8,128)}, u32[]{:S(2)}) copy-start(f32[1,448,2048]{2,1,0:T(8,128)} %param.5) | copy-start | bytes 11010052
  45.3 153.4 %all-reduce.3.cloned.1.call-start = ((), (), s32[]{:S(2)}) async-start(), calls=%async_computation.3 | async-start | bytes 2097152 | tf_op jit(solution)/shard_map/psum | solution.py:63
  104.4 280.5 %reduce-scatter.3.cloned.1.call-start = ((), (), s32[]{:S(2)}) async-start(), calls=%async_computation.4 | async-start | bytes 2621440 | tf_op jit(solution)/shard_map/reduce_scatter | solution.py:40
  201.7 1.0 copy-start.4
  341.9 7.2 %copy-start.1 = (f32[1,448,2048]{2,1,0:T(8,128)S(1)}, f32[1,448,2048]{2,1,0:T(8,128)}, u32[]{:S(2)}) copy-start(f32[1,448,2048]{2,1,0:T(8,128)} %param.5) | copy-start | bytes 11010052
  351.7 57.2 %reduce-scatter.5.cloned.1.call-start = ((), (), s32[]{:S(2)}) async-start(), calls=%async_computation.5 | async-start | bytes 655360 | tf_op jit(solution)/shard_map/reduce_scatter | solution.py:40
  384.9 67.7 %all-gather.10.cloned.1.call-start = ((), (), s32[]{:S(2)}) async-start(), calls=%async_computation.8 | async-start | bytes 2228224 | tf_op jit(solution)/shard_map/all_gather | solution.py:34
  409.0 118.2 %all-gather.6.cloned.1.call-start = ((), (), s32[]{:S(2)}) async-start(), calls=%async_computation.6 | async-start | bytes 4456448 | tf_op jit(solution)/shard_map/all_gather | solution.py:78
  527.1 4.5 copy-start.2
  531.6 2.9 copy-start.5
Sparse Core Ops, SparseCore 0:
  45.4 51.7 all-gather.7
  104.5 94.1 all-reduce.2
  351.9 33.0 reduce-scatter.2
  387.3 21.5 reduce-scatter.4
  410.6 41.9 all-gather.9
  473.1 53.9 all-gather.5
where the time goes:
time: 548 us; the launch traced here: 543 us
  waiting for transfers between devices  300 us (55%)
  other arithmetic  135 us (25%)
  blocking collectives  51.6 us (9%)
  matrix products  24.6 us (4%)
  between operations  17.2 us (3%)
  local copies, waits for them, and re-layouts  14.5 us (3%)
    all_gather x2, waiting for transfers between devices, gathered_total(): return lax.all_gather(value, axis).astype(jnp.float32).sum(0)  95.5 us
    psum x1, waiting for transfers between devices, per_device(): lax.psum(jnp.dot(left_mean.T, left_mean, precision=lax.Precision.HIGHEST)...  92.8 us
    another operation x14, other arithmetic, per_device(): chol = jnp.linalg.cholesky(gram)  78.8 us
    reduce_scatter x2, waiting for transfers between devices, sum_by_axis(): running = lax.psum_scatter(running, axis, scatter_dimension=0, tiled=True)  57.1 us
    all_gather x1, waiting for transfers between devices, per_device(): lax.all_gather(stacked, ROWS, axis=1, tiled=True)  54.2 us
    another operation x3, other arithmetic, per_device(): jax.scipy.linalg.solve_triangular(chol, left_mean.T, lower=True)  40.4 us
    all_to_all x1, blocking collectives, from_everyone(): lax.all_to_all(jnp.broadcast_to(value[None], (size, *value.shape)), axis,...  34.8 us
    psum x2, blocking collectives, over_axes(): value = lax.psum(value, axis)  16.8 us
  transfers between devices with their start and end apart: 6, of which 6 were waited for; matrix products, arithmetic and copies ran while one was open for 0% of the time, Pallas kernels for 0%

commit v1 on v0

--- a/solution.py
+++ b/solution.py
@@ -75,7 +75,7 @@
     both = jnp.einsum(
         "ir,skr->sik",
         left_half,
-        lax.all_gather(stacked, ROWS, axis=1, tiled=True),
+        jnp.concatenate(lax.all_gather(stacked, ROWS), axis=1),
         preferred_element_type=jnp.float32,
     )
     feedback = both[0]

time: 548 us -> 548 us (level)
  no operation moved by 1% of the time
where the time goes in v1:
time: 548 us; the launch traced here: 544 us
  waiting for transfers between devices  300 us (55%)
  other arithmetic  135 us (25%)
  blocking collectives  51.6 us (9%)
  matrix products  22.3 us (4%)
  between operations  17.2 us (3%)
  local copies, waits for them, and re-layouts  17 us (3%)
    all_gather x2, waiting for transfers between devices, gathered_total(): return lax.all_gather(value, axis).astype(jnp.float32).sum(0)  95.5 us
    psum x1, waiting for transfers between devices, per_device(): lax.psum(jnp.dot(left_mean.T, left_mean, precision=lax.Precision.HIGHEST)...  92.8 us
    another operation x14, other arithmetic, per_device(): chol = jnp.linalg.cholesky(gram)  78.8 us
    reduce_scatter x2, waiting for transfers between devices, sum_by_axis(): running = lax.psum_scatter(running, axis, scatter_dimension=0, tiled=True)  57.1 us
    all_gather x1, waiting for transfers between devices, per_device(): lax.all_gather(stacked, ROWS)  54.1 us
    another operation x3, other arithmetic, per_device(): jax.scipy.linalg.solve_triangular(chol, left_mean.T, lower=True)  40.4 us
    all_to_all x1, blocking collectives, from_everyone(): lax.all_to_all(jnp.broadcast_to(value[None], (size, *value.shape)), axis,...  34.8 us
    psum x2, blocking collectives, over_axes(): value = lax.psum(value, axis)  16.8 us
  transfers between devices with their start and end apart: 6, of which 6 were waited for; matrix products, arithmetic and copies ran while one was open for 0% of the time, Pallas kernels for 0%

profile of v1, /device:TPU:1, one launch (start us, length us, event | category | flops | bytes accessed | tf_op | source)
XLA Modules:
  0.0 543.6 jit_solution(10056313816332258750)
XLA Ops:
  7.2 1.1 convert_element_type.64
  8.4 0.2 broadcast_in_dim.3
  8.6 34.8 %all_to_all.5 = bf16[16,128,512]{2,1,0:T(8,128)(2,1)S(1)} all-to-all(bf16[16,128,512]{2,1,0:T(8,128)(2,1)S(1)} %broadcast_in_dim.3), channel_id=1, replica_groups=mesh['rep'=16,'rows_0'=4,'rows_1'=4] {'rows_0','rows_1'}, dimensions={0} | all-to-all | bytes 4194304 | tf_op jit(solution)/shard_map/all_to_all | solution.py:17
  43.3 1.9 convolution_convert_fusion.1
  45.4 51.9 %all-gather.7.cloned.1.call-done = bf16[7168,512]{1,0:T(8,128)(2,1)} async-done(((bf16[448,512]{1,0:T(8,128)(2,1)}), bf16[7168,512]{1,0:T(8,128)(2,1)}) %all-gather.7.cloned.1.call-update) | async-done | bytes 7340048 | tf_op jit(solution)/shard_map/all_gather | solution.py:34
  97.2 4.2 convert_reduce_fusion
  101.4 2.9 fusion.7
  104.4 0.5 reduce-scatter.3.cloned.1.call-start
  104.9 1.0 multiply_bitcast_fusion
  105.9 92.8 %all-reduce.3.cloned.1.call-done = f32[512,512]{0,1:T(8,128)} async-done(((f32[512,512]{0,1:T(8,128)}), f32[512,512]{0,1:T(8,128)}) %all-reduce.3.cloned.1.call-update) | async-done | bytes 1048592 | tf_op jit(solution)/shard_map/psum | solution.py:63
  198.7 1.6 copy.11
  200.3 1.4 fusion.6
  201.8 1.0 copy-done.4
  202.7 11.7 %cholesky.104 = f32[128,128]{1,0:T(8,128)S(1)} custom-call(f32[128,128]{1,0:T(8,128)S(1)} %cholesky.266), custom_call_target="Cholesky" | custom-call | tf_op jit(solution)/shard_map/jit(cholesky)/cholesky | solution.py:64
  214.5 9.8 %custom-call.31 = f32[1,128,128]{1,2,0:T(8,128)S(1)} custom-call(f32[1,128,128]{2,1,0:T(8,128)S(1)} %get-tuple-element.32), custom_call_target="InvertDiagBlocksLowerTriangular" | custom-call | tf_op jit(solution)/shard_map/jit(cholesky)/cholesky | solution.py:64
  224.3 0.1 cholesky.224
  224.4 1.2 constant_dynamic-update-slice_fusion.3
  225.7 1.3 convolution_subtract_fusion.3
  227.0 11.7 %cholesky.217 = f32[128,128]{1,0:T(8,128)S(1)} custom-call(f32[128,128]{1,0:T(8,128)S(1)} %cholesky.270), custom_call_target="Cholesky" | custom-call | tf_op jit(solution)/shard_map/jit(cholesky)/cholesky | solution.py:64
  238.7 10.0 %custom-call.32 = f32[1,128,128]{1,2,0:T(8,128)S(1)} custom-call(f32[1,128,128]{2,1,0:T(8,128)S(1)} %get-tuple-element.29), custom_call_target="InvertDiagBlocksLowerTriangular" | custom-call | tf_op jit(solution)/shard_map/jit(cholesky)/cholesky | solution.py:64
  248.7 0.3 convolution_dynamic-update-slice_fusion
  248.9 1.3 convolution_subtract_fusion.4
  250.2 11.7 %cholesky.238 = f32[128,128]{1,0:T(8,128)S(1)} custom-call(f32[128,128]{1,0:T(8,128)S(1)} %cholesky.275), custom_call_target="Cholesky" | custom-call | tf_op jit(solution)/shard_map/jit(cholesky)/cholesky | solution.py:64
  262.0 0.7 compare_reduce_fusion.1
  262.7 9.8 %custom-call.33 = f32[1,128,128]{1,2,0:T(8,128)S(1)} custom-call(f32[1,128,128]{2,1,0:T(8,128)S(1)} %get-tuple-element.26), custom_call_target="InvertDiagBlocksLowerTriangular" | custom-call | tf_op jit(solution)/shard_map/jit(cholesky)/cholesky | solution.py:64
  272.5 0.2 convolution_dynamic-update-slice_fusion.1
  272.7 1.2 convolution_subtract_fusion.5
  273.9 11.7 %cholesky.255 = f32[128,128]{1,0:T(8,128)S(1)} custom-call(f32[128,128]{1,0:T(8,128)S(1)} %convolution_subtract_fusion.5), custom_call_target="Cholesky" | custom-call | tf_op jit(solution)/shard_map/jit(cholesky)/cholesky | solution.py:64
  285.7 0.6 compare_reduce_fusion
  286.3 0.9 compare_reduce_fusion.2
  289.7 1.1 select_select_fusion
  290.8 11.7 %while.1 = (s32[]{:T(128)}, f32[512,512]{1,0:T(8,128)}, s32[4,2]{0,1:T(2,128)S(1)}, f32[4,128,128]{2,1,0:T(8,128)S(1)}, s32[]{:T(128)}) while((s32[]{:T(128)}, f32[512,512]{1,0:T(8,128)}, s32[4,2]{0,1:T(2,128)S(1)}, f32[4,128,128]{2,1,0:T(8,128)S(1)}, s32[]{:T(128)}) %tuple.35), condition=%wide.while_cond, body=%wide.while_body.sunk | while | flops 2 | bytes 131189 | solution.py:65
  290.8 0.1 constant_dynamic-slice_fusion.2
  290.9 0.6 fusion.57
  291.5 2.2 bitcast_dynamic-update-slice_fusion.2
  293.9 0.6 fusion.57
  294.5 2.2 bitcast_dynamic-update-slice_fusion.2
  296.8 0.6 fusion.57
  297.4 2.2 bitcast_dynamic-update-slice_fusion.2
  299.7 0.1 constant_dynamic-slice_fusion.2
  299.7 0.6 fusion.57
  300.3 2.2 bitcast_dynamic-update-slice_fusion.2
  302.5 39.3 %custom-call.34 = f32[4,128,128]{1,2,0:T(8,128)S(1)} custom-call(f32[4,128,128]{2,1,0:T(8,128)S(1)} %get-tuple-element.10), custom_call_target="InvertDiagBlocksLowerTriangular" | custom-call | tf_op jit(solution)/shard_map/jit(_solve_triangular)/triangular_solve | solution.py:65
  341.9 1.4 fusion.48
  343.3 1.3 convolution_subtract_fusion.2
  344.6 0.3 fusion.47
  345.0 1.5 convolution_subtract_fusion.1
  346.5 0.3 fusion.46
  346.9 1.8 convolution_subtract_fusion
  348.7 0.3 convolution_convert_fusion.2
  349.0 2.7 convolution_convert_fusion
  351.8 33.1 %reduce-scatter.3.cloned.1.call-done = bf16[512,512]{1,0:T(8,128)(2,1)} async-done(((bf16[2048,512]{1,0:T(8,128)(2,1)}), bf16[512,512]{1,0:T(8,128)(2,1)}) %reduce-scatter.3.cloned.1.call-update) | async-done | bytes 524304 | tf_op jit(solution)/shard_map/reduce_scatter | solution.py:40
  385.0 23.9 %reduce-scatter.5.cloned.1.call-done = bf16[128,512]{1,0:T(8,128)(2,1)} async-done(((bf16[512,512]{1,0:T(8,128)(2,1)}), bf16[128,512]{1,0:T(8,128)(2,1)}) %reduce-scatter.5.cloned.1.call-update) | async-done | bytes 131088 | tf_op jit(solution)/shard_map/reduce_scatter | solution.py:40
  409.0 43.6 %all-gather.9.cloned.1.call-done = bf16[2048,512]{1,0:T(8,128)(2,1)} async-done(((bf16[128,512]{1,0:T(8,128)(2,1)}), bf16[2048,512]{1,0:T(8,128)(2,1)}) %all-gather.9.cloned.1.call-update) | async-done | bytes 2097168 | tf_op jit(solution)/shard_map/all_gather | solution.py:34
  452.6 1.9 convert_reduce_fusion.1
  454.6 8.5 %psum.22 = f32[512]{0:T(512)S(1)} all-reduce(f32[512]{0:T(512)S(1)} %multiply_reduce_fusion), channel_id=1, replica_groups=mesh['rep'=16,'rows_0'=4,'rows_1'=4] {'rows_0'}, use_global_device_ids=true, to_apply=%region_14.15 | all-reduce | flops 512 | bytes 4096 | tf_op jit(solution)/shard_map/psum | solution.py:46
  463.0 8.4 %psum.23 = f32[512]{0:T(512)S(1)} all-reduce(f32[512]{0:T(512)S(1)} %psum.22), channel_id=1, replica_groups=mesh['rep'=16,'rows_0'=4,'rows_1'=4] {'rows_1'}, use_global_device_ids=true, to_apply=%region_15.16 | all-reduce | flops 512 | bytes 4096 | tf_op jit(solution)/shard_map/psum | solution.py:46
  471.5 0.7 multiply_divide_fusion
  472.2 0.7 pad_maximum_fusion.1
  473.0 54.1 %all-gather.11.cloned.1.call-done = bf16[32,128,512]{2,1,0:T(8,128)(2,1)} async-done(((bf16[2,128,512]{2,1,0:T(8,128)(2,1)}), bf16[32,128,512]{2,1,0:T(8,128)(2,1)}) %all-gather.11.cloned.1.call-update) | async-done | bytes 4194320 | tf_op jit(solution)/shard_map/all_gather | solution.py:78
  527.1 2.5 copy.12
  529.6 2.2 convolution_bitcast_fusion
  531.8 2.9 fusion
  534.6 1.9 fusion.3
  (37 shorter events, 0.7 us)
Async XLA Ops:
  7.2 36.2 %copy-start.3 = (bf16[1,448,2048]{2,1,0:T(8,128)(2,1)S(1)}, bf16[1,448,2048]{2,1,0:T(8,128)(2,1)}, u32[]{:S(2)}) copy-start(bf16[1,448,2048]{2,1,0:T(8,128)(2,1)} %param.6) | copy-start | bytes 5505028
  7.2 90.1 %all-gather.7.cloned.1.call-start = ((), (), s32[]{:S(2)}) async-start(), calls=%async_computation.6 | async-start | bytes 7798784 | tf_op jit(solution)/shard_map/all_gather | solution.py:34
  7.2 36.1 %copy-start = (f32[1,448,2048]{2,1,0:T(8,128)S(1)}, f32[1,448,2048]{2,1,0:T(8,128)}, u32[]{:S(2)}) copy-start(f32[1,448,2048]{2,1,0:T(8,128)} %param.5) | copy-start | bytes 11010052
  45.3 153.4 %all-reduce.3.cloned.1.call-start = ((), (), s32[]{:S(2)}) async-start(), calls=%async_computation.3 | async-start | bytes 2097152 | tf_op jit(solution)/shard_map/psum | solution.py:63
  104.4 280.5 %reduce-scatter.3.cloned.1.call-start = ((), (), s32[]{:S(2)}) async-start(), calls=%async_computation.4 | async-start | bytes 2621440 | tf_op jit(solution)/shard_map/reduce_scatter | solution.py:40
  201.7 1.0 copy-start.4
  341.9 7.2 %copy-start.1 = (f32[1,448,2048]{2,1,0:T(8,128)S(1)}, f32[1,448,2048]{2,1,0:T(8,128)}, u32[]{:S(2)}) copy-start(f32[1,448,2048]{2,1,0:T(8,128)} %param.5) | copy-start | bytes 11010052
  351.7 57.2 %reduce-scatter.5.cloned.1.call-start = ((), (), s32[]{:S(2)}) async-start(), calls=%async_computation.5 | async-start | bytes 655360 | tf_op jit(solution)/shard_map/reduce_scatter | solution.py:40
  384.9 67.7 %all-gather.9.cloned.1.call-start = ((), (), s32[]{:S(2)}) async-start(), calls=%async_computation.7 | async-start | bytes 2228224 | tf_op jit(solution)/shard_map/all_gather | solution.py:34
  409.0 118.2 %all-gather.11.cloned.1.call-start = ((), (), s32[]{:S(2)}) async-start(), calls=%async_computation.8 | async-start | bytes 4456448 | tf_op jit(solution)/shard_map/all_gather | solution.py:78
  529.6 2.2 copy-start.2
  531.8 2.9 copy-start.5
Sparse Core Ops, SparseCore 0:
  45.4 51.7 all-gather.6
  104.5 94.1 all-reduce.2
  351.9 33.0 reduce-scatter.2
  387.3 21.5 reduce-scatter.4
  410.6 41.9 all-gather.8
  473.1 53.9 all-gather.10
